TPU v7x, 32 devices: a whole 2x2x4 slice. The times are simulated.
32 devices in a mesh: seq: 4 (over y, x), fsdp: 8 (over z, core).
Axes of the slice: x: 2, y: 2, z: 4, core: 2. Of those that a mesh axis runs over, the one named last changes fastest.
Arguments:
- block_input: bfloat16 [8, 2048, 1024], P('fsdp', 'seq'), may hold values from -6 to 6
- norm_gain_a: float32 [1024], P('fsdp'), may hold values from 0.1 to 1.9
- weight_qkv: float32 [1024, 3072], P('fsdp'), may hold values from -0.1875 to 0.1875
- weight_out: float32 [1024, 1024], P('fsdp'), may hold values from -3 to 3
- norm_gain_b: float32 [1024], P('fsdp'), may hold values from 0.1 to 1.9
- weight_gate_up: float32 [1024, 8192], P('fsdp'), may hold values from -0.1875 to 0.1875
- weight_down: float32 [1024, 4096], P('fsdp'), may hold values from -0.09375 to 0.09375
- cotangent: bfloat16 [8, 2048, 1024], P('fsdp', 'seq'), may hold values from -6 to 6
- permutation: int32 [8, 2048], P('fsdp'), may hold values from 0 to 2047, each once within a row
- lengths: int32 [8, 3], P('fsdp'), may hold values from 256 to 1024, as said below
- offsets: int32 [8, 3], P('fsdp'), may hold values from 0 to 1792, as said below
Outputs:
- block_output: bfloat16 [8, 2048, 1024], P('fsdp', 'seq')
- grad_input: bfloat16 [8, 2048, 1024], P('fsdp', 'seq')
- grad_gain_a: float32 [1024], P('fsdp')
- grad_qkv: float32 [1024, 3072], P('fsdp')
- grad_out: float32 [1024, 1024], P('fsdp')
- grad_gain_b: float32 [1024], P('fsdp')
- grad_gate_up: float32 [1024, 8192], P('fsdp')
- grad_down: float32 [1024, 4096], P('fsdp')
Inputs may be any that keep to these rules, and one draw needn't show every extreme that they name: A group's 3 lengths sum to 2048, and its longest is exactly 1024. offsets[g, k] is the sum of lengths[g, i] over i < k, so that a group's sequences tile its positions.
All inputs are finite; a program needn't handle non-finite values.
Results may differ from a plain program's by a relative error of at most 0.02.
Values may be sent and summed in bfloat16 or wider, within the bound.
A program may use at most 256 MiB of HBM per device.

v0:
```python
import jax
import jax.numpy as jnp
from jax import lax
from jax.sharding import PartitionSpec as P

HEADS = 16
HEAD_DIM = 64
epsilon = 1e-05


def rms_scale(values):
    return lax.rsqrt(jnp.mean(values * values, axis=-1, keepdims=True) + epsilon)


def norm_backward(values, inv_scale, grad_normed, gain):
    scaled = grad_normed * gain
    gain_grad = jnp.sum(grad_normed * values * inv_scale, axis=0)
    input_grad = inv_scale * scaled - values * inv_scale**3 * jnp.mean(
        values * scaled, axis=-1, keepdims=True
    )
    return (input_grad, gain_grad)


def block_mask(seg_query, pos_query, segment, position):
    return (seg_query[:, None] == segment[None, :]) & (position[None, :] <= pos_query[:, None])


def on_device(
    block_input,
    norm_gain_a,
    weight_qkv,
    weight_out,
    norm_gain_b,
    weight_gate_up,
    weight_down,
    cotangent,
    permutation,
    lengths,
    offsets,
):
    seq_count = lax.axis_size("seq")
    row_count = block_input.shape[1]
    model_width = block_input.shape[2]
    group_len = row_count * seq_count
    head_local = HEADS // seq_count
    score_scale = HEAD_DIM ** (-0.5)
    blk_rows = min(512, group_len)
    block_count = group_len // blk_rows
    inputs = block_input[0].astype(jnp.float32)
    gain_a, full_qkv, full_out = (
        lax.all_gather(norm_gain_a.astype(jnp.bfloat16), "fsdp", axis=0, tiled=True),
        lax.all_gather(weight_qkv.astype(jnp.bfloat16), "fsdp", axis=0, tiled=True),
        lax.all_gather(weight_out.astype(jnp.bfloat16), "fsdp", axis=0, tiled=True),
    )
    inv_first = rms_scale(inputs)
    normed_a = (inputs * inv_first * gain_a.astype(jnp.float32)).astype(jnp.bfloat16)
    qkv_rows = jnp.dot(normed_a, full_qkv, preferred_element_type=jnp.float32).astype(jnp.bfloat16)
    head_rows = lax.all_to_all(
        qkv_rows.reshape(row_count, 3, seq_count, -1),
        "seq",
        split_axis=2,
        concat_axis=0,
        tiled=True,
    )
    head_rows = head_rows.reshape(group_len, 3, head_local, HEAD_DIM)
    position = jnp.arange(group_len, dtype=jnp.int32)
    dealt_pos = permutation[0]
    inverse = jnp.zeros((group_len,), jnp.int32).at[dealt_pos].set(position)
    ordered = head_rows[inverse]
    seq_starts = offsets[0]
    seq_lengths = lengths[0]
    inside = (position[:, None] >= seq_starts[None, :]) & (
        position[:, None] < seq_starts[None, :] + seq_lengths[None, :]
    )
    segment = jnp.sum(
        inside.astype(jnp.int32) * jnp.arange(seq_lengths.shape[0], dtype=jnp.int32)[None, :],
        axis=1,
    )
    queries = ordered[:, 0]
    key_rows = ordered[:, 1]
    values = ordered[:, 2]

    def forward_block(block_item):
        query_blk, seg_blk, pos_blk = block_item
        scores = (
            jnp.einsum("qhd,khd->hqk", query_blk, key_rows, preferred_element_type=jnp.float32)
            * score_scale
        )
        allowed = block_mask(seg_blk, pos_blk, segment, position)
        scores = jnp.where(allowed[None], scores, -1e30)
        row_top = jnp.max(scores, axis=-1, keepdims=True)
        exponent = jnp.exp(scores - row_top)
        row_total = jnp.sum(exponent, axis=-1, keepdims=True)
        weights_low = (exponent / row_total).astype(jnp.bfloat16)
        attended = jnp.einsum(
            "hqk,khd->qhd", weights_low, values, preferred_element_type=jnp.float32
        )
        return (attended.astype(jnp.bfloat16), (row_top + jnp.log(row_total))[:, :, 0])

    query_blocks = queries.reshape(block_count, blk_rows, head_local, HEAD_DIM)
    seg_blocks = segment.reshape(block_count, blk_rows)
    pos_blocks = position.reshape(block_count, blk_rows)
    attended, log_total = lax.map(forward_block, (query_blocks, seg_blocks, pos_blocks))
    dealt_out = attended.reshape(group_len, -1)[dealt_pos]
    mixed = lax.all_to_all(
        dealt_out.reshape(group_len, 1, -1), "seq", split_axis=0, concat_axis=1, tiled=True
    ).reshape(row_count, model_width)
    hidden = inputs + jnp.dot(mixed, full_out, preferred_element_type=jnp.float32)
    gain_b, full_gate_up, full_down = (
        lax.all_gather(norm_gain_b.astype(jnp.bfloat16), "fsdp", axis=0, tiled=True),
        lax.all_gather(weight_gate_up.astype(jnp.bfloat16), "fsdp", axis=0, tiled=True),
        lax.all_gather(weight_down.astype(jnp.bfloat16), "fsdp", axis=0, tiled=True),
    )
    inv_second = rms_scale(hidden)
    normed_b = (hidden * inv_second * gain_b.astype(jnp.float32)).astype(jnp.bfloat16)
    gate_up = jnp.dot(normed_b, full_gate_up, preferred_element_type=jnp.float32)
    hidden_units = full_gate_up.shape[1] // 2
    gate_part = gate_up[:, :hidden_units]
    up_part = gate_up[:, hidden_units:]
    gate_sigmoid = jax.nn.sigmoid(gate_part)
    gate_silu = gate_part * gate_sigmoid
    activation = (gate_silu * up_part).astype(jnp.bfloat16)
    branch_out = jnp.einsum("rf,df->rd", activation, full_down, preferred_element_type=jnp.float32)
    result_rows = (hidden + branch_out).astype(jnp.bfloat16)
    gain_b, full_gate_up, full_down = (
        lax.all_gather(norm_gain_b.astype(jnp.bfloat16), "fsdp", axis=0, tiled=True),
        lax.all_gather(weight_gate_up.astype(jnp.bfloat16), "fsdp", axis=0, tiled=True),
        lax.all_gather(weight_down.astype(jnp.bfloat16), "fsdp", axis=0, tiled=True),
    )
    out_grad = cotangent[0].astype(jnp.float32)
    out_grad_low = out_grad.astype(jnp.bfloat16)
    grad_down_term = jnp.einsum(
        "rd,rf->df", out_grad_low, activation, preferred_element_type=jnp.float32
    )
    grad_activation = jnp.dot(out_grad_low, full_down, preferred_element_type=jnp.float32)
    grad_gate = grad_activation * up_part * gate_sigmoid * (1.0 + gate_part * (1.0 - gate_sigmoid))
    grad_up = grad_activation * gate_silu
    grad_gate_up = jnp.concatenate([grad_gate, grad_up], axis=1).astype(jnp.bfloat16)
    grad_gate_up_term = jnp.einsum(
        "rd,rf->df", normed_b, grad_gate_up, preferred_element_type=jnp.float32
    )
    grad_normed_b = jnp.einsum(
        "rf,df->rd", grad_gate_up, full_gate_up, preferred_element_type=jnp.float32
    )
    hidden_back, grad_gain_b_term = norm_backward(
        hidden, inv_second, grad_normed_b, gain_b.astype(jnp.float32)
    )
    grad_hidden = out_grad + hidden_back
    gain_a, full_qkv, full_out = (
        lax.all_gather(norm_gain_a.astype(jnp.bfloat16), "fsdp", axis=0, tiled=True),
        lax.all_gather(weight_qkv.astype(jnp.bfloat16), "fsdp", axis=0, tiled=True),
        lax.all_gather(weight_out.astype(jnp.bfloat16), "fsdp", axis=0, tiled=True),
    )
    grad_branch = grad_hidden.astype(jnp.bfloat16)
    grad_out_term = jnp.einsum("rd,re->de", mixed, grad_branch, preferred_element_type=jnp.float32)
    grad_mixed = jnp.einsum(
        "re,de->rd", grad_branch, full_out, preferred_element_type=jnp.float32
    ).astype(jnp.bfloat16)
    grad_heads = lax.all_to_all(
        grad_mixed.reshape(row_count, seq_count, -1), "seq", split_axis=1, concat_axis=0, tiled=True
    )
    grad_ordered = grad_heads.reshape(group_len, head_local, HEAD_DIM)[inverse]
    grad_blocks = grad_ordered.reshape(block_count, blk_rows, head_local, HEAD_DIM)

    def backward_block(carry, block_item):
        key_acc, value_acc = carry
        query_blk, grad_blk, log_blk, seg_blk, pos_blk = block_item
        scores = (
            jnp.einsum("qhd,khd->hqk", query_blk, key_rows, preferred_element_type=jnp.float32)
            * score_scale
        )
        allowed = block_mask(seg_blk, pos_blk, segment, position)
        scores = jnp.where(allowed[None], scores, -1e30)
        probability = jnp.exp(scores - log_blk[:, :, None])
        grad_prob = jnp.einsum("qhd,khd->hqk", grad_blk, values, preferred_element_type=jnp.float32)
        row_delta = jnp.sum(probability * grad_prob, axis=-1, keepdims=True)
        grad_score = (probability * (grad_prob - row_delta)).astype(jnp.bfloat16)
        grad_query = (
            jnp.einsum("hqk,khd->qhd", grad_score, key_rows, preferred_element_type=jnp.float32)
            * score_scale
        )
        key_acc = (
            key_acc
            + jnp.einsum("hqk,qhd->khd", grad_score, query_blk, preferred_element_type=jnp.float32)
            * score_scale
        )
        value_acc = value_acc + jnp.einsum(
            "hqk,qhd->khd",
            probability.astype(jnp.bfloat16),
            grad_blk,
            preferred_element_type=jnp.float32,
        )
        return ((key_acc, value_acc), grad_query.astype(jnp.bfloat16))

    zero_acc = jnp.zeros((group_len, head_local, HEAD_DIM), jnp.float32)
    accumulated, query_grad = lax.scan(
        backward_block,
        (zero_acc, zero_acc),
        (query_blocks, grad_blocks, log_total, seg_blocks, pos_blocks),
    )
    qkv_grad = jnp.stack(
        [
            query_grad.reshape(group_len, -1),
            accumulated[0].reshape(group_len, -1).astype(jnp.bfloat16),
            accumulated[1].reshape(group_len, -1).astype(jnp.bfloat16),
        ],
        axis=1,
    )
    dealt_grad = qkv_grad[dealt_pos]
    rows_grad = lax.all_to_all(
        dealt_grad.reshape(group_len, 3, 1, -1), "seq", split_axis=0, concat_axis=2, tiled=True
    ).reshape(row_count, -1)
    grad_qkv_term = jnp.einsum("rd,re->de", normed_a, rows_grad, preferred_element_type=jnp.float32)
    grad_normed_a = jnp.einsum("re,de->rd", rows_grad, full_qkv, preferred_element_type=jnp.float32)
    input_back, grad_gain_a_term = norm_backward(
        inputs, inv_first, grad_normed_a, gain_a.astype(jnp.float32)
    )
    input_grad = (grad_hidden + input_back).astype(jnp.bfloat16)
    attn_shards = (
        lax.psum_scatter(
            grad_gain_a_term.astype(jnp.bfloat16), "fsdp", scatter_dimension=0, tiled=True
        ).astype(jnp.float32),
        lax.psum_scatter(
            grad_qkv_term.astype(jnp.bfloat16), "fsdp", scatter_dimension=0, tiled=True
        ).astype(jnp.float32),
        lax.psum_scatter(
            grad_out_term.astype(jnp.bfloat16), "fsdp", scatter_dimension=0, tiled=True
        ).astype(jnp.float32),
    )
    mlp_shards = (
        lax.psum_scatter(
            grad_gain_b_term.astype(jnp.bfloat16), "fsdp", scatter_dimension=0, tiled=True
        ).astype(jnp.float32),
        lax.psum_scatter(
            grad_gate_up_term.astype(jnp.bfloat16), "fsdp", scatter_dimension=0, tiled=True
        ).astype(jnp.float32),
        lax.psum_scatter(
            grad_down_term.astype(jnp.bfloat16), "fsdp", scatter_dimension=0, tiled=True
        ).astype(jnp.float32),
    )
    totals = (
        lax.psum(attn_shards[0].astype(jnp.bfloat16), "seq").astype(jnp.float32),
        lax.psum(attn_shards[1].astype(jnp.bfloat16), "seq").astype(jnp.float32),
        lax.psum(attn_shards[2].astype(jnp.bfloat16), "seq").astype(jnp.float32),
        lax.psum(mlp_shards[0].astype(jnp.bfloat16), "seq").astype(jnp.float32),
        lax.psum(mlp_shards[1].astype(jnp.bfloat16), "seq").astype(jnp.float32),
        lax.psum(mlp_shards[2].astype(jnp.bfloat16), "seq").astype(jnp.float32),
    )
    return (
        result_rows[None],
        input_grad[None],
        totals[0],
        totals[1],
        totals[2],
        totals[3],
        totals[4],
        totals[5],
    )


def solution(mesh):
    placed = (
        P("fsdp", "seq", None),
        P("fsdp"),
        P("fsdp", None),
        P("fsdp", None),
        P("fsdp"),
        P("fsdp", None),
        P("fsdp", None),
        P("fsdp", "seq", None),
        P("fsdp", None),
        P("fsdp", None),
        P("fsdp", None),
    )
    return jax.shard_map(
        on_device,
        mesh=mesh,
        in_specs=placed,
        out_specs=(
            P("fsdp", "seq", None),
            P("fsdp", "seq", None),
            P("fsdp"),
            P("fsdp", None),
            P("fsdp", None),
            P("fsdp"),
            P("fsdp", None),
            P("fsdp", None),
        ),
        check_vma=False,
    )
```

profile of v0, /device:TPU:0, one launch (start us, length us, event | category | flops | bytes accessed | tf_op | source)
XLA Modules:
  0.0 1127.1 jit_solution(276207675843231154)
XLA Ops:
  15.4 13.5 %all-gather = bf16[8,1,128]{2,1,0:T(2,128)(2,1)S(1)} all-gather(bf16[1,1,128]{2,1,0:T(2,128)(2,1)S(1)} %convert_bitcast_fusion.3), channel_id=1, replica_groups=mesh['seq'=4,'fsdp'=8] {'fsdp'}, dimensions={0}, use_global_device_ids=true | all-gather | bytes 2304 | tf_op jit(solution)/shard_map/all_gather | solution.py:51
  29.8 47.9 %all-gather.7.cloned.1.call-done = bf16[1024,3072]{1,0:T(8,128)(2,1)} async-done(((bf16[128,3072]{1,0:T(8,128)(2,1)}), bf16[1024,3072]{1,0:T(8,128)(2,1)}) %all-gather.7.cloned.1.call-update) | async-done | bytes 6291472 | tf_op jit(solution)/shard_map/all_gather | solution.py:52
  77.7 7.7 convolution_convert_fusion.2
  85.4 5.5 reshape.321
  102.6 8.5 scatter_custom_fusion
  112.3 23.5 %all-to-all-done = bf16[512,3,4,256]{0,3,1,2:T(8,128)(2,1)S(1)} async-done(((bf16[512,3,4,256]{0,3,1,2:T(8,128)(2,1)}), bf16[512,3,4,256]{0,3,1,2:T(8,128)(2,1)S(1)}, u32[]{:S(2)}, u32[]{:S(2)}) %all-to-all-start) | async-done | bytes 3145760 | tf_op jit(solution)/shard_map/all_to_all | solution.py:58
  135.8 4.6 copy.141
  140.4 13.1 %reshape.380 = bf16[2048,3,4,64]{3,2,1,0:T(4,128)(2,1)} reshape(bf16[4,512,3,1,256]{4,2,1,0,3:T(4,128)(2,1)} %copy.141) | data formatting | bytes 6291456 | tf_op jit(solution)/shard_map/reshape | solution.py:65
  153.6 23.0 %gather_fusion = bf16[2048,3,4,64]{3,2,1,0:T(4,128)(2,1)} fusion(bf16[2048,3,4,64]{3,2,1,0:T(4,128)(2,1)} %reshape.380, s32[2048]{0:T(1024)S(1)} %fusion.84), kind=kCustom, calls=%fused_computation | custom fusion | bytes 6299648 | tf_op jit(solution)/shard_map/gather | solution.py:69
  176.5 5.4 slice_bitcast_fusion
  191.8 64.2 %while.28 = (s32[]{:T(128)}, bf16[4,512,4,64]{1,3,2,0:T(8,128)(2,1)}, f32[4,4,512]{2,1,0:T(4,128)}, s32[4,512]{1,0:T(4,128)}, s32[2048]{0:T(1024)S(1)}, /*index=...) while((s32[]{:T(128)}, ...), condition=%wide.region_6.7_spmd.clone, body=%wide.region_3.6_spmd.clone.sunk | while | flops 1127348224 | bytes 57233532 | solution.py:103
  197.0 4.3 fusion.135
  201.3 5.9 fusion.136
  213.1 4.3 fusion.135
  217.4 5.9 fusion.136
  229.1 4.3 fusion.135
  233.4 5.9 fusion.136
  249.5 5.9 fusion.136
  264.6 9.1 gather_fusion.1
  282.9 9.8 all-gather.1
  305.5 4.5 multiply_reduce_fusion.3
  310.1 18.8 %fusion.89 = f32[512,8192]{1,0:T(8,128)} fusion(bf16[1024,8192]{1,0:T(8,128)(2,1)} %all-gather.11.cloned.1.call-done, f32[512,1024]{1,0:T(8,128)} %get-tuple-element.422, f32[1024]{0:T(1024)S(1)} %bitcast.234, f32[512]{0:T(512)S(1)} %get-tuple-element.420), kind=kOutput, calls=%fused_computation.139 | convolution fusion | flops 8591507456 | bytes 35657728 | tf_op jit(solution)/shard_map/dot_general | solution.py:116
  328.9 13.4 %all-gather.13.cloned.1.call-done = bf16[1024,4096]{1,0:T(8,128)(2,1)} async-done(((bf16[128,4096]{1,0:T(8,128)(2,1)}), bf16[1024,4096]{1,0:T(8,128)(2,1)}) %all-gather.13.cloned.1.call-update) | async-done | bytes 8388624 | tf_op jit(solution)/shard_map/all_gather | solution.py:112
  342.3 15.1 %multiply_convert_fusion.2 = (bf16[512,4096]{1,0:T(8,128)(2,1)}, bf16[512,4096]{1,0:T(8,128)(2,1)}, bf16[512,4096]{1,0:T(8,128)(2,1)S(1)}) fusion(f32[512,8192]{1,0:T(8,128)} %fusion.89, bf16[1024,4096]{1,0:T(8,128)(2,1)} %all-gather.13.cloned.1.call-done, bf16[1,512,1024]{2,1,0:T(8,128)(2,1)S(1)} %copy-done.22), kind=kOutput, calls=%fused_computation.67 | convolution fusion | flops 4326424576 | bytes 38797312 | tf_op jit(solution)/shard_map/dot_general | solution.py:135
  359.4 6.8 convert_bitcast_fusion
  366.2 11.7 %copy.151 = bf16[1024,4096]{1,0:T(8,128)(2,1)} copy(bf16[1024,4096]{0,1:T(8,128)(2,1)} %convert_bitcast_fusion) | data formatting | bytes 16777216
  377.9 18.0 %multiply_reduce_fusion.1 = (bf16[1024]{0:T(1024)(128)(2,1)}, f32[512]{0:T(512)S(1)}, f32[512,1024]{1,0:T(8,128)}) fusion(f32[512,1024]{1,0:T(8,128)} %get-tuple-element.422, f32[512]{0:T(512)S(1)} %get-tuple-element.420, f32[1024]{0:T(1024)S(1)} %bitcast.235, bf16[1024,8192]{1,0:T(8,128)(2,1)} %all-gather.11.cloned.1.call-done, ...), kind=kOutput, calls=%fused_computation.97 | convolution fusion | flops 8609855488 | bytes 29370368 | tf_op jit(solution)/shard_map/rf,df->rd/dot_general | solution.py:142
  406.6 4.5 convolution_convert_fusion.3
  411.2 9.6 all-to-all-done.2
  425.0 16.1 %gather_fusion.2 = bf16[2048,4,64]{2,1,0:T(4,128)(2,1)} fusion(bf16[2048,4,64]{2,1,0:T(4,128)(2,1)} %reshape.382, s32[2048]{0:T(1024)S(1)} %copy-done.27), kind=kCustom, calls=%fused_computation.2 | custom fusion | bytes 2105344 | tf_op jit(solution)/shard_map/gather | solution.py:162
  446.2 209.1 %while.29 = (s32[]{:T(128)}, f32[2048,4,64]{0,2,1:T(8,128)}, f32[2048,4,64]{0,2,1:T(8,128)}, bf16[4,512,4,64]{1,3,2,0:T(8,128)(2,1)}, bf16[4,512,4,64]{1,3,2,0:T...) while((s32[]{:T(128)}, f32[2048,4,64]{0,2,1:T(8,128)}, ...), condition=%wide.region_11.12_spmd.clone, body=%wide.region_9.11_spmd.clone.sunk | while | flops 2753296384 | bytes 268841472 | solution.py:196
  454.4 12.3 %multiply_reduce_fusion.5 = (f32[4,512]{1,0:T(4,128)}, f32[4,512,2048]{2,1,0:T(8,128)}) fusion(f32[4,512,2048]{2,1,0:T(8,128)S(1)} %fusion.146, f32[4,512]{1,0:T(4,128)S(1)} %dynamic-slice_bitcast_fusion.2, pred[512,2048]{1,0:T(8,128)(4,1)S(1)} %fusion.147, bf16[2048,4,64]{0,2,1:T(8,128)(2,1)} %get-tuple-element.638, ...), kind=kOutput, calls=%fused_computation.28.clone.1 | convolution fusion | flops 557840384 | bytes 35930116 | tf_op jit(solution)/shard_map/while/body/eval_jaxpr/qhd,khd->hqk/dot_general | solution.py:175
  466.7 11.0 multiply_convert_fusion.8
  477.7 6.7 fusion.148
  484.4 8.6 fusion.149
  493.1 5.4 fusion.150
  506.3 12.3 %multiply_reduce_fusion.5 = (f32[4,512]{1,0:T(4,128)}, f32[4,512,2048]{2,1,0:T(8,128)}) fusion(f32[4,512,2048]{2,1,0:T(8,128)S(1)} %fusion.146, f32[4,512]{1,0:T(4,128)S(1)} %dynamic-slice_bitcast_fusion.2, pred[512,2048]{1,0:T(8,128)(4,1)S(1)} %fusion.147, bf16[2048,4,64]{0,2,1:T(8,128)(2,1)} %get-tuple-element.638, ...), kind=kOutput, calls=%fused_computation.28.clone.1 | convolution fusion | flops 557840384 | bytes 35930116 | tf_op jit(solution)/shard_map/while/body/eval_jaxpr/qhd,khd->hqk/dot_general | solution.py:175
  518.6 10.9 multiply_convert_fusion.8
  529.6 7.2 fusion.148
  536.8 8.5 fusion.149
  545.3 5.4 fusion.150
  558.5 12.3 %multiply_reduce_fusion.5 = (f32[4,512]{1,0:T(4,128)}, f32[4,512,2048]{2,1,0:T(8,128)}) fusion(f32[4,512,2048]{2,1,0:T(8,128)S(1)} %fusion.146, f32[4,512]{1,0:T(4,128)S(1)} %dynamic-slice_bitcast_fusion.2, pred[512,2048]{1,0:T(8,128)(4,1)S(1)} %fusion.147, bf16[2048,4,64]{0,2,1:T(8,128)(2,1)} %get-tuple-element.638, ...), kind=kOutput, calls=%fused_computation.28.clone.1 | convolution fusion | flops 557840384 | bytes 35930116 | tf_op jit(solution)/shard_map/while/body/eval_jaxpr/qhd,khd->hqk/dot_general | solution.py:175
  570.8 10.9 multiply_convert_fusion.8
  581.8 7.2 fusion.148
  589.0 8.5 fusion.149
  597.5 5.4 fusion.150
  610.7 12.3 %multiply_reduce_fusion.5 = (f32[4,512]{1,0:T(4,128)}, f32[4,512,2048]{2,1,0:T(8,128)}) fusion(f32[4,512,2048]{2,1,0:T(8,128)S(1)} %fusion.146, f32[4,512]{1,0:T(4,128)S(1)} %dynamic-slice_bitcast_fusion.2, pred[512,2048]{1,0:T(8,128)(4,1)S(1)} %fusion.147, bf16[2048,4,64]{0,2,1:T(8,128)(2,1)} %get-tuple-element.638, ...), kind=kOutput, calls=%fused_computation.28.clone.1 | convolution fusion | flops 557840384 | bytes 35930116 | tf_op jit(solution)/shard_map/while/body/eval_jaxpr/qhd,khd->hqk/dot_general | solution.py:175
  623.0 10.9 multiply_convert_fusion.8
  634.0 7.2 fusion.148
  641.2 8.5 fusion.149
  649.7 5.4 fusion.150
  669.0 8.2 reshape.383
  677.3 9.5 pad_maximum_fusion.3
  686.7 18.7 %gather_fusion.3 = bf16[2048,3,256]{2,1,0:T(4,128)(2,1)} fusion(bf16[2048,3,256]{2,1,0:T(4,128)(2,1)} %pad_maximum_fusion.3, s32[2048]{0:T(1024)S(1)} %copy-done.25), kind=kCustom, calls=%fused_computation.3 | custom fusion | bytes 6299648 | tf_op jit(solution)/shard_map/gather | solution.py:209
  705.4 51.5 %all_to_all.60 = bf16[2048,3,1,256]{3,1,2,0:T(4,128)(2,1)S(1)} all-to-all(bf16[2048,3,1,256]{3,1,2,0:T(4,128)(2,1)} %bitcast.213), channel_id=1, replica_groups=mesh['seq'=4,'fsdp'=8] {'seq'}, dimensions={0} | all-to-all | bytes 6291456 | tf_op jit(solution)/shard_map/all_to_all | solution.py:210
  760.2 8.5 convolution_convert_fusion.1
  770.4 16.6 %convolution_convert_fusion = bf16[1024,8192]{1,0:T(8,128)(2,1)} fusion(bf16[512,4096]{1,0:T(8,128)(2,1)} %get-tuple-element.412, bf16[512,4096]{1,0:T(8,128)(2,1)} %get-tuple-element.411, f32[512,1024]{1,0:T(8,128)S(1)} %copy-done.12, f32[1024]{0:T(1024)S(1)} %bitcast.237, f32[512]{0:T(512)S(1)} %copy-done.36), kind=kOutput, calls=%fused_computation.63 | convolution fusion | flops 8616673280 | bytes 27269120 | tf_op jit(solution)/shard_map/rd,rf->df/dot_general | solution.py:139
  789.6 45.9 %reduce-scatter.7.cloned.1.call-done = bf16[128,3072]{1,0:T(8,128)(2,1)} async-done(((bf16[1024,3072]{1,0:T(8,128)(2,1)}), bf16[128,3072]{1,0:T(8,128)(2,1)}) %reduce-scatter.7.cloned.1.call-update) | async-done | bytes 786448 | tf_op jit(solution)/shard_map/reduce_scatter | solution.py:223
  835.4 169.0 %reduce-scatter.11.cloned.1.call-done = bf16[128,8192]{1,0:T(8,128)(2,1)} async-done(((bf16[1024,8192]{1,0:T(8,128)(2,1)}), bf16[128,8192]{1,0:T(8,128)(2,1)}) %reduce-scatter.11.cloned.1.call-update) | async-done | bytes 2097168 | tf_op jit(solution)/shard_map/reduce_scatter | solution.py:234
  1005.7 10.3 fusion.69
  1016.0 8.0 fusion.66
  1024.0 13.6 %all-reduce.2 = (bf16[1024]{0:T(1024)(128)(2,1)S(1)}, bf16[1024]{0:T(1024)(128)(2,1)S(1)}) all-reduce(bf16[1024]{0:T(1024)(128)(2,1)S(1)} %get-tuple-element.351, bf16[1024]{0:T(1024)(128)(2,1)S(1)} %copy-done.38), channel_id=2, replica_groups=mesh['seq'=4,'fsdp'=8] {'fsdp'}, use_global_device_ids=true, to_apply=%region_14.15.clone | all-reduce | flops 2048 | bytes 8192
  1037.8 10.2 all-reduce.3
  1052.1 59.8 %all-reduce.7.cloned.1.call-done = (bf16[128,4096]{0,1:T(8,128)(2,1)}, bf16[128,3072]{1,0:T(8,128)(2,1)}, bf16[128,1024]{1,0:T(8,128)(2,1)}, bf16[128,8192]{1,0:T(8,128)(2,1)}) async-done(((bf16[128,4096]{0,1:T(8,128)(2,1)}, bf16[128,3072]{1,0:T(8,128)(2,1)}, bf16[128,1024]{1,0:T(8,128)(2,1)}, bf16[128,8192]{1,0:T(8,128)(2,1)}), (bf16[128,4096]{0,1:T(8,128)(2,1)}, bf16[128,3072]{1,0:T(8,128)(2,1)}, ...) | async-done | bytes 4194320 | tf_op jit(solution)/shard_map/psum | solution.py:247
  (285 shorter events, 177.5 us)
Async XLA Ops:
  7.2 70.6 %all-gather.7.cloned.1.call-start = ((), (), s32[]{:S(2)}) async-start(), calls=%async_computation.8 | async-start | bytes 7077888 | tf_op jit(solution)/shard_map/all_gather | solution.py:52
  9.6 295.9 %all-gather.9.cloned.1.call-start = ((), (), s32[]{:S(2)}) async-start(), calls=%async_computation.9 | async-start | bytes 2359296 | tf_op jit(solution)/shard_map/all_gather | solution.py:53
  11.5 17.4 %copy-start.7 = (bf16[1,512,1024]{2,1,0:T(8,128)(2,1)S(1)}, bf16[1,512,1024]{2,1,0:T(8,128)(2,1)}, u32[]{:S(2)}) copy-start(bf16[1,512,1024]{2,1,0:T(8,128)(2,1)} %param.15) | copy-start | bytes 3145732
  11.5 298.6 %all-gather.11.cloned.1.call-start = ((), (), s32[]{:S(2)}) async-start(), calls=%async_computation.10 | async-start | bytes 18874368 | tf_op jit(solution)/shard_map/all_gather | solution.py:111
  28.9 48.8 %copy-start.30 = (f32[8,1,128]{2,1,0:T(1,128)}, f32[8,1,128]{2,1,0:T(1,128)S(1)}, u32[]{:S(2)}) copy-start(f32[8,1,128]{2,1,0:T(1,128)S(1)} %convert_element_type.214) | copy-start | bytes 12292
  29.8 47.9 %copy-start.33 = (f32[512]{0:T(512)}, f32[512]{0:T(512)S(1)}, u32[]{:S(2)}) copy-start(f32[512]{0:T(512)S(1)} %get-tuple-element.418) | copy-start | bytes 6148
  95.2 6.7 copy-start.39
  95.2 6.7 copy-start.41
  95.2 7.4 copy-start.37
  95.2 40.6 %all-to-all-start = ((bf16[512,3,4,256]{0,3,1,2:T(8,128)(2,1)}), bf16[512,3,4,256]{0,3,1,2:T(8,128)(2,1)S(1)}, u32[]{:S(2)}, u32[]{:S(2)}) async-start(bf16[512,3,4,256]{0,3,1,2:T(8,128)(2,1)} %copy.114), calls=%async_computation | async-start | bytes 6291456 | tf_op jit(solution)/shard_map/all_to_all | solution.py:58
  99.1 243.2 %all-gather.13.cloned.1.call-start = ((), (), s32[]{:S(2)}) async-start(), calls=%async_computation.11 | async-start | bytes 9437184 | tf_op jit(solution)/shard_map/all_gather | solution.py:112
  112.3 41.2 %copy-start.26 = (s32[2048]{0:T(1024)}, s32[2048]{0:T(1024)S(1)}, u32[]{:S(2)}) copy-start(s32[2048]{0:T(1024)S(1)} %fusion.84) | copy-start | bytes 24580
  256.1 8.6 copy-start.24
  273.7 9.2 copy-start.42
  278.5 17.8 %all-to-all-start.1 = ((bf16[4,2,65536]{2,1,0:T(2,128)(2,1)}), bf16[4,2,65536]{2,1,0:T(2,128)(2,1)}, u32[]{:S(2)}, u32[]{:S(2)}) async-start(bf16[4,2,65536]{2,1,0:T(2,128)(2,1)} %reshape.393), calls=%async_computation.1 | async-start | bytes 2097152 | tf_op jit(solution)/shard_map/all_to_all | solution.py:105
  282.8 504.3 %reduce-scatter.13.cloned.1.call-start = ((), (), s32[]{:S(2)}) async-start(), calls=%async_computation.15 | async-start | bytes 9437184
  292.7 103.2 %copy-start.28 = (f32[8,1,128]{2,1,0:T(1,128)}, f32[8,1,128]{2,1,0:T(1,128)S(1)}, u32[]{:S(2)}) copy-start(f32[8,1,128]{2,1,0:T(1,128)S(1)} %convert_element_type.215) | copy-start | bytes 12292
  292.7 12.8 %copy-start.8 = (bf16[1,512,1024]{2,1,0:T(8,128)(2,1)S(1)}, bf16[1,512,1024]{2,1,0:T(8,128)(2,1)}, u32[]{:S(2)}) copy-start(bf16[1,512,1024]{2,1,0:T(8,128)(2,1)} %param.15) | copy-start | bytes 3145732
  310.0 85.9 %copy-start.35 = (f32[512]{0:T(512)}, f32[512]{0:T(512)S(1)}, u32[]{:S(2)}) copy-start(f32[512]{0:T(512)S(1)} %get-tuple-element.420) | copy-start | bytes 6148
  310.1 32.2 %copy-start.22 = (bf16[1,512,1024]{2,1,0:T(8,128)(2,1)S(1)}, bf16[1,512,1024]{2,1,0:T(8,128)(2,1)}, u32[]{:S(2)}) copy-start(bf16[1,512,1024]{2,1,0:T(8,128)(2,1)} %param.22) | copy-start | bytes 3145732
  402.8 17.9 %all-to-all-start.2 = ((bf16[512,4,256]{0,2,1:T(8,128)(2,1)}), bf16[512,4,256]{0,2,1:T(8,128)(2,1)S(1)}, u32[]{:S(2)}, u32[]{:S(2)}) async-start(bf16[512,4,256]{0,2,1:T(8,128)(2,1)} %bitcast.222), calls=%async_computation.2 | async-start | bytes 2097152 | tf_op jit(solution)/shard_map/all_to_all | solution.py:159
  406.5 383.0 %reduce-scatter.9.cloned.1.call-start = ((), (), s32[]{:S(2)}) async-start(), calls=%async_computation.13 | async-start | bytes 2359296 | tf_op jit(solution)/shard_map/reduce_scatter | solution.py:226
  411.1 13.9 %copy-start.27 = (s32[2048]{0:T(1024)S(1)}, s32[2048]{0:T(1024)}, u32[]{:S(2)}) copy-start(s32[2048]{0:T(1024)} %copy-done.26) | copy-start | bytes 24580
  411.1 424.3 %reduce-scatter.7.cloned.1.call-start = ((), (), s32[]{:S(2)}) async-start(), calls=%async_computation.12 | async-start | bytes 7077888 | tf_op jit(solution)/shard_map/reduce_scatter | solution.py:223
  450.9 15.8 %copy-start = (f32[4,512,2048]{2,1,0:T(8,128)}, f32[4,512,2048]{2,1,0:T(8,128)S(1)}, u32[]{:S(2)}) copy-start(f32[4,512,2048]{2,1,0:T(8,128)S(1)} %fusion.146) | copy-start | bytes 50331652 | tf_op jit(solution)/shard_map/while
  477.7 6.7 copy-start.17
  477.7 15.3 %slice-start = ((s8[8388608]{0:T(1024)(128)(4,1)}), s8[4194304]{0:T(1024)(128)(4,1)S(1)}, s32[]{:S(2)}) async-start(s8[8388608]{0:T(1024)(128)(4,1)} %bitcast.211), calls=%async_computation.17 | async-start | bytes 8388608 | tf_op jit(solution)/shard_map/while
  484.4 8.6 slice-start.1
  493.0 5.4 copy-start.18
  493.1 5.4 copy-start.2
  493.1 5.4 copy-start.6
  493.1 5.4 copy-start.21
  502.8 15.8 %copy-start = (f32[4,512,2048]{2,1,0:T(8,128)}, f32[4,512,2048]{2,1,0:T(8,128)S(1)}, u32[]{:S(2)}) copy-start(f32[4,512,2048]{2,1,0:T(8,128)S(1)} %fusion.146) | copy-start | bytes 50331652 | tf_op jit(solution)/shard_map/while
  529.5 7.2 copy-start.17
  529.5 15.7 %slice-start = ((s8[8388608]{0:T(1024)(128)(4,1)}), s8[4194304]{0:T(1024)(128)(4,1)S(1)}, s32[]{:S(2)}) async-start(s8[8388608]{0:T(1024)(128)(4,1)} %bitcast.211), calls=%async_computation.17 | async-start | bytes 8388608 | tf_op jit(solution)/shard_map/while
  536.8 8.5 slice-start.1
  545.2 5.4 copy-start.18
  545.3 5.4 copy-start.2
  545.3 5.4 copy-start.6
  555.0 15.8 %copy-start = (f32[4,512,2048]{2,1,0:T(8,128)}, f32[4,512,2048]{2,1,0:T(8,128)S(1)}, u32[]{:S(2)}) copy-start(f32[4,512,2048]{2,1,0:T(8,128)S(1)} %fusion.146) | copy-start | bytes 50331652 | tf_op jit(solution)/shard_map/while
  581.7 7.2 copy-start.17
  581.8 15.7 %slice-start = ((s8[8388608]{0:T(1024)(128)(4,1)}), s8[4194304]{0:T(1024)(128)(4,1)S(1)}, s32[]{:S(2)}) async-start(s8[8388608]{0:T(1024)(128)(4,1)} %bitcast.211), calls=%async_computation.17 | async-start | bytes 8388608 | tf_op jit(solution)/shard_map/while
  589.0 8.5 slice-start.1
  597.4 5.4 copy-start.18
  597.5 5.4 copy-start.2
  597.5 5.4 copy-start.6
  607.2 15.8 %copy-start = (f32[4,512,2048]{2,1,0:T(8,128)}, f32[4,512,2048]{2,1,0:T(8,128)S(1)}, u32[]{:S(2)}) copy-start(f32[4,512,2048]{2,1,0:T(8,128)S(1)} %fusion.146) | copy-start | bytes 50331652 | tf_op jit(solution)/shard_map/while
  634.0 7.2 copy-start.17
  634.0 15.7 %slice-start = ((s8[8388608]{0:T(1024)(128)(4,1)}), s8[4194304]{0:T(1024)(128)(4,1)S(1)}, s32[]{:S(2)}) async-start(s8[8388608]{0:T(1024)(128)(4,1)} %bitcast.211), calls=%async_computation.17 | async-start | bytes 8388608 | tf_op jit(solution)/shard_map/while
  641.2 8.5 slice-start.1
  649.7 5.4 copy-start.18
  649.7 5.4 copy-start.2
  655.3 5.7 copy-start.3
  664.8 12.4 %copy-start.13 = (bf16[2048,1,256]{2,1,0:T(2,128)(2,1)S(1)}, bf16[2048,1,256]{2,1,0:T(2,128)(2,1)}, u32[]{:S(2)}) copy-start(bf16[2048,1,256]{2,1,0:T(2,128)(2,1)} %copy.136) | copy-start | bytes 3145732
  677.3 9.5 copy-start.25
  768.8 235.6 %reduce-scatter.11.cloned.1.call-start = ((), (), s32[]{:S(2)}) async-start(), calls=%async_computation.14 | async-start | bytes 18874368 | tf_op jit(solution)/shard_map/reduce_scatter | solution.py:234
  787.0 217.4 %copy-start.43 = (u32[32]{0:T(128)S(1)}, u32[32]{0:T(128)}, u32[]{:S(2)}) copy-start(u32[32]{0:T(128)} %constant.73) | copy-start | bytes 388
  787.0 324.9 %all-reduce.7.cloned.1.call-start = ((), (), s32[]{:S(2)}) async-start(), calls=%async_computation.16 | async-start | bytes 8388608 | tf_op jit(solution)/shard_map/psum | solution.py:247
  1005.7 10.3 copy-start.9
  1005.7 10.3 copy-start.15
  1016.0 8.0 copy-start.38
  1016.0 33.0 %copy-start.11 = (f32[512,1024]{1,0:T(8,128)S(1)}, f32[512,1024]{1,0:T(8,128)}, u32[]{:S(2)}) copy-start(f32[512,1024]{1,0:T(8,128)} %copy-done.10) | copy-start | bytes 6291460
  1016.0 33.0 %copy-start.32 = (f32[512]{0:T(512)S(1)}, f32[512]{0:T(512)}, u32[]{:S(2)}) copy-start(f32[512]{0:T(512)} %get-tuple-element.417) | copy-start | bytes 6148
  1111.9 6.8 copy-start.23
  (28 other events, 88.2 us)
Sparse Core Ops, SparseCore 0:
  10.2 67.4 all-gather.6
  79.9 27.7 all-gather.8
  109.3 150.5 all-gather.10
  261.9 80.2 all-gather.12
  378.0 88.1 reduce-scatter.12
  468.4 34.2 reduce-scatter.8
  768.9 66.4 reduce-scatter.6
  837.8 166.5 reduce-scatter.10
  1008.7 103.2 all-reduce.6
where the time goes:
time: 1140 us; the launch traced here: 1130 us
  waiting for transfers between devices  373 us (33%)
  matrix products  303 us (27%)
  local copies, waits for them, and re-layouts  207 us (18%)
  other arithmetic  117 us (10%)
  blocking collectives  98.6 us (9%)
  between operations  15.1 us (1%)
  starting transfers between devices  12.2 us (1%)
    reduce_scatter x1, waiting for transfers between devices, on_device(): lax.psum_scatter(grad_gate_up_term.astype(jnp.bfloat16), 'fsdp', scatter_...  169 us
    psum x1, waiting for transfers between devices, on_device(): lax.psum(mlp_shards[2].astype(jnp.bfloat16), 'seq').astype(jnp.float32)  59.8 us
    all_to_all x1, blocking collectives, on_device(): lax.all_to_all(dealt_grad.reshape(group_len, 3, 1, -1), 'seq', split_axis...  51.5 us
    dot_general x4, matrix products, backward_block(): jnp.einsum('qhd,khd->hqk', grad_blk, values, preferred_element_type=jnp.f...  49.3 us
    all_gather x1, waiting for transfers between devices, on_device(): lax.all_gather(weight_qkv.astype(jnp.bfloat16), 'fsdp', axis=0, tiled=True)  47.9 us
    reduce_scatter x1, waiting for transfers between devices, on_device(): lax.psum_scatter(grad_qkv_term.astype(jnp.bfloat16), 'fsdp', scatter_dime...  45.9 us
    unnamed x85, local copies, waits for them, and re-layouts  44.8 us
    convert_element_type x4, other arithmetic, backward_block(): grad_score = (probability * (grad_prob - row_delta)).astype(jnp.bfloat16)  43.7 us
  transfers between devices with their start and end apart: 12, of which 8 were waited for; matrix products, arithmetic and copies ran while one was open for 51% of the time, Pallas kernels for 0%

commit v1 on v0

--- a/solution.py
+++ b/solution.py
@@ -244,7 +244,9 @@
         lax.psum(attn_shards[2].astype(jnp.bfloat16), "seq").astype(jnp.float32),
         lax.psum(mlp_shards[0].astype(jnp.bfloat16), "seq").astype(jnp.float32),
         lax.psum(mlp_shards[1].astype(jnp.bfloat16), "seq").astype(jnp.float32),
-        lax.psum(mlp_shards[2].astype(jnp.bfloat16), "seq").astype(jnp.float32),
+        jnp.sum(lax.all_gather(mlp_shards[2].astype(jnp.bfloat16), "seq"), axis=0).astype(
+            jnp.float32
+        ),
     )
     return (
         result_rows[None],

time: 1140 us -> 1170 us (1.026)
  other arithmetic: 117 us -> 140 us
    reduce_sum x0 -> x1, other arithmetic: none -> 23 us  [on_device(): jnp.sum(lax.all_gather(mlp_shards[2].astype(jnp.bfloat16), 'seq'), axis=0)]
    unnamed x85 -> x83, local copies, waits for them, and re-layouts: 44.8 us -> 44.5 us
  transfers between devices with their start and end apart: 12 -> 13, of which waited for: 8 -> 9; matrix products, arithmetic and copies ran while one was open for 51% -> 52% of each run, Pallas kernels for 0% -> 0%
where the time goes in v1:
time: 1170 us; the launch traced here: 1160 us
  waiting for transfers between devices  378 us (32%)
  matrix products  304 us (26%)
  local copies, waits for them, and re-layouts  213 us (18%)
  other arithmetic  140 us (12%)
  blocking collectives  99.2 us (8%)
  between operations  15.4 us (1%)
  starting transfers between devices  12.2 us (1%)
    reduce_scatter x1, waiting for transfers between devices, on_device(): lax.psum_scatter(grad_gate_up_term.astype(jnp.bfloat16), 'fsdp', scatter_...  169 us
    psum x1, waiting for transfers between devices, on_device(): lax.psum(attn_shards[1].astype(jnp.bfloat16), 'seq').astype(jnp.float32)  59.3 us
    all_to_all x1, blocking collectives, on_device(): lax.all_to_all(dealt_grad.reshape(group_len, 3, 1, -1), 'seq', split_axis...  51.6 us
    dot_general x4, matrix products, backward_block(): jnp.einsum('qhd,khd->hqk', grad_blk, values, preferred_element_type=jnp.f...  49.3 us
    all_gather x1, waiting for transfers between devices, on_device(): lax.all_gather(weight_qkv.astype(jnp.bfloat16), 'fsdp', axis=0, tiled=True)  47.9 us
    unnamed x83, local copies, waits for them, and re-layouts  44.5 us
    reduce_scatter x1, waiting for transfers between devices, on_device(): lax.psum_scatter(grad_qkv_term.astype(jnp.bfloat16), 'fsdp', scatter_dime...  44.4 us
    convert_element_type x4, other arithmetic, backward_block(): grad_score = (probability * (grad_prob - row_delta)).astype(jnp.bfloat16)  43.8 us
  transfers between devices with their start and end apart: 13, of which 9 were waited for; matrix products, arithmetic and copies ran while one was open for 52% of the time, Pallas kernels for 0%

profile of v1, /device:TPU:0, one launch (start us, length us, event | category | flops | bytes accessed | tf_op | source)
XLA Modules:
  0.0 1162.7 jit_solution(18437802570399786372)
XLA Ops:
  15.4 13.5 %all-gather.1 = bf16[8,1,128]{2,1,0:T(2,128)(2,1)S(1)} all-gather(bf16[1,1,128]{2,1,0:T(2,128)(2,1)S(1)} %convert_bitcast_fusion.3), channel_id=1, replica_groups=mesh['seq'=4,'fsdp'=8] {'fsdp'}, dimensions={0}, use_global_device_ids=true | all-gather | bytes 2304 | tf_op jit(solution)/shard_map/all_gather | solution.py:51
  29.8 47.9 %all-gather.9.cloned.1.call-done = bf16[1024,3072]{1,0:T(8,128)(2,1)} async-done(((bf16[128,3072]{1,0:T(8,128)(2,1)}), bf16[1024,3072]{1,0:T(8,128)(2,1)}) %all-gather.9.cloned.1.call-update) | async-done | bytes 6291472 | tf_op jit(solution)/shard_map/all_gather | solution.py:52
  77.7 7.7 convolution_convert_fusion.2
  85.4 5.5 reshape.321
  102.6 8.2 scatter_custom_fusion
  112.0 23.8 %all-to-all-done = bf16[512,3,4,256]{0,3,1,2:T(8,128)(2,1)S(1)} async-done(((bf16[512,3,4,256]{0,3,1,2:T(8,128)(2,1)}), bf16[512,3,4,256]{0,3,1,2:T(8,128)(2,1)S(1)}, u32[]{:S(2)}, u32[]{:S(2)}) %all-to-all-start) | async-done | bytes 3145760 | tf_op jit(solution)/shard_map/all_to_all | solution.py:58
  135.8 4.6 copy.138
  140.4 13.1 %reshape.381 = bf16[2048,3,4,64]{3,2,1,0:T(4,128)(2,1)} reshape(bf16[4,512,3,1,256]{4,2,1,0,3:T(4,128)(2,1)} %copy.138) | data formatting | bytes 6291456 | tf_op jit(solution)/shard_map/reshape | solution.py:65
  153.6 23.0 %gather_fusion = bf16[2048,3,4,64]{3,2,1,0:T(4,128)(2,1)} fusion(bf16[2048,3,4,64]{3,2,1,0:T(4,128)(2,1)} %reshape.381, s32[2048]{0:T(1024)S(1)} %fusion.84), kind=kCustom, calls=%fused_computation | custom fusion | bytes 6299648 | tf_op jit(solution)/shard_map/gather | solution.py:69
  176.6 5.4 slice_bitcast_fusion
  191.8 64.2 %while.28 = (s32[]{:T(128)}, bf16[4,512,4,64]{1,3,2,0:T(8,128)(2,1)}, f32[4,4,512]{2,1,0:T(4,128)}, s32[4,512]{1,0:T(4,128)}, s32[2048]{0:T(1024)S(1)}, /*index=...) while((s32[]{:T(128)}, ...), condition=%wide.region_6.7_spmd.clone, body=%wide.region_3.6_spmd.clone.sunk | while | flops 1127348224 | bytes 57233532 | solution.py:103
  201.4 5.9 fusion.136
  217.4 5.9 fusion.136
  233.5 5.9 fusion.136
  249.5 5.9 fusion.136
  264.6 9.1 gather_fusion.1
  282.9 9.7 all-gather.2
  305.6 4.5 multiply_reduce_fusion.3
  310.2 18.8 %fusion.89 = f32[512,8192]{1,0:T(8,128)} fusion(bf16[1024,8192]{1,0:T(8,128)(2,1)} %all-gather.13.cloned.1.call-done, f32[512,1024]{1,0:T(8,128)} %get-tuple-element.397, f32[1024]{0:T(1024)S(1)} %bitcast.236, f32[512]{0:T(512)S(1)} %get-tuple-element.395), kind=kOutput, calls=%fused_computation.139 | convolution fusion | flops 8591507456 | bytes 35657728 | tf_op jit(solution)/shard_map/dot_general | solution.py:116
  329.0 13.3 %all-gather.15.cloned.1.call-done = bf16[1024,4096]{1,0:T(8,128)(2,1)} async-done(((bf16[128,4096]{1,0:T(8,128)(2,1)}), bf16[1024,4096]{1,0:T(8,128)(2,1)}) %all-gather.15.cloned.1.call-update) | async-done | bytes 8388624 | tf_op jit(solution)/shard_map/all_gather | solution.py:112
  342.3 15.1 %multiply_convert_fusion.2 = (bf16[512,4096]{1,0:T(8,128)(2,1)}, bf16[512,4096]{1,0:T(8,128)(2,1)}, bf16[512,4096]{1,0:T(8,128)(2,1)S(1)}) fusion(f32[512,8192]{1,0:T(8,128)} %fusion.89, bf16[1024,4096]{1,0:T(8,128)(2,1)} %all-gather.15.cloned.1.call-done, bf16[1,512,1024]{2,1,0:T(8,128)(2,1)S(1)} %copy-done.22), kind=kOutput, calls=%fused_computation.67 | convolution fusion | flops 4326424576 | bytes 38797312 | tf_op jit(solution)/shard_map/dot_general | solution.py:135
  359.4 6.8 convert_bitcast_fusion
  366.2 11.5 copy.148
  377.8 18.2 %multiply_reduce_fusion.1 = (bf16[1024]{0:T(1024)(128)(2,1)}, f32[512]{0:T(512)S(1)}, f32[512,1024]{1,0:T(8,128)}) fusion(f32[512,1024]{1,0:T(8,128)} %get-tuple-element.397, f32[512]{0:T(512)S(1)} %get-tuple-element.395, f32[1024]{0:T(1024)S(1)} %bitcast.237, bf16[1024,8192]{1,0:T(8,128)(2,1)} %all-gather.13.cloned.1.call-done, ...), kind=kOutput, calls=%fused_computation.97 | convolution fusion | flops 8609855488 | bytes 29370368 | tf_op jit(solution)/shard_map/rf,df->rd/dot_general | solution.py:142
  406.6 4.5 convolution_convert_fusion.3
  411.2 9.6 all-to-all-done.2
  425.1 16.1 %gather_fusion.2 = bf16[2048,4,64]{2,1,0:T(4,128)(2,1)} fusion(bf16[2048,4,64]{2,1,0:T(4,128)(2,1)} %reshape.383, s32[2048]{0:T(1024)S(1)} %copy-done.26), kind=kCustom, calls=%fused_computation.2 | custom fusion | bytes 2105344 | tf_op jit(solution)/shard_map/gather | solution.py:162
  446.3 208.9 %while.29 = (s32[]{:T(128)}, f32[2048,4,64]{0,2,1:T(8,128)}, f32[2048,4,64]{0,2,1:T(8,128)}, bf16[4,512,4,64]{1,3,2,0:T(8,128)(2,1)}, bf16[4,512,4,64]{1,3,2,0:T...) while((s32[]{:T(128)}, f32[2048,4,64]{0,2,1:T(8,128)}, ...), condition=%wide.region_11.12_spmd.clone, body=%wide.region_9.11_spmd.clone.sunk | while | flops 2753296384 | bytes 268841472 | solution.py:196
  454.2 12.3 %multiply_reduce_fusion.5 = (f32[4,512]{1,0:T(4,128)}, f32[4,512,2048]{2,1,0:T(8,128)}) fusion(f32[4,512,2048]{2,1,0:T(8,128)S(1)} %fusion.146, f32[4,512]{1,0:T(4,128)S(1)} %dynamic-slice_bitcast_fusion.2, pred[512,2048]{1,0:T(8,128)(4,1)S(1)} %fusion.147, bf16[2048,4,64]{0,2,1:T(8,128)(2,1)} %get-tuple-element.613, ...), kind=kOutput, calls=%fused_computation.28.clone.1 | convolution fusion | flops 557840384 | bytes 35930116 | tf_op jit(solution)/shard_map/while/body/eval_jaxpr/qhd,khd->hqk/dot_general | solution.py:175
  466.6 11.0 multiply_convert_fusion.8
  477.5 6.7 fusion.148
  484.2 8.6 fusion.149
  492.9 5.4 fusion.150
  506.1 12.3 %multiply_reduce_fusion.5 = (f32[4,512]{1,0:T(4,128)}, f32[4,512,2048]{2,1,0:T(8,128)}) fusion(f32[4,512,2048]{2,1,0:T(8,128)S(1)} %fusion.146, f32[4,512]{1,0:T(4,128)S(1)} %dynamic-slice_bitcast_fusion.2, pred[512,2048]{1,0:T(8,128)(4,1)S(1)} %fusion.147, bf16[2048,4,64]{0,2,1:T(8,128)(2,1)} %get-tuple-element.613, ...), kind=kOutput, calls=%fused_computation.28.clone.1 | convolution fusion | flops 557840384 | bytes 35930116 | tf_op jit(solution)/shard_map/while/body/eval_jaxpr/qhd,khd->hqk/dot_general | solution.py:175
  518.5 10.9 multiply_convert_fusion.8
  529.4 7.2 fusion.148
  536.6 8.5 fusion.149
  545.1 5.4 fusion.150
  558.3 12.3 %multiply_reduce_fusion.5 = (f32[4,512]{1,0:T(4,128)}, f32[4,512,2048]{2,1,0:T(8,128)}) fusion(f32[4,512,2048]{2,1,0:T(8,128)S(1)} %fusion.146, f32[4,512]{1,0:T(4,128)S(1)} %dynamic-slice_bitcast_fusion.2, pred[512,2048]{1,0:T(8,128)(4,1)S(1)} %fusion.147, bf16[2048,4,64]{0,2,1:T(8,128)(2,1)} %get-tuple-element.613, ...), kind=kOutput, calls=%fused_computation.28.clone.1 | convolution fusion | flops 557840384 | bytes 35930116 | tf_op jit(solution)/shard_map/while/body/eval_jaxpr/qhd,khd->hqk/dot_general | solution.py:175
  570.7 10.9 multiply_convert_fusion.8
  581.6 7.2 fusion.148
  588.8 8.5 fusion.149
  597.4 5.4 fusion.150
  610.5 12.3 %multiply_reduce_fusion.5 = (f32[4,512]{1,0:T(4,128)}, f32[4,512,2048]{2,1,0:T(8,128)}) fusion(f32[4,512,2048]{2,1,0:T(8,128)S(1)} %fusion.146, f32[4,512]{1,0:T(4,128)S(1)} %dynamic-slice_bitcast_fusion.2, pred[512,2048]{1,0:T(8,128)(4,1)S(1)} %fusion.147, bf16[2048,4,64]{0,2,1:T(8,128)(2,1)} %get-tuple-element.613, ...), kind=kOutput, calls=%fused_computation.28.clone.1 | convolution fusion | flops 557840384 | bytes 35930116 | tf_op jit(solution)/shard_map/while/body/eval_jaxpr/qhd,khd->hqk/dot_general | solution.py:175
  622.9 10.9 multiply_convert_fusion.8
  633.8 7.2 fusion.148
  641.0 8.5 fusion.149
  649.6 5.4 fusion.150
  668.9 8.2 reshape.384
  677.1 9.5 pad_maximum_fusion.3
  686.6 18.7 %gather_fusion.3 = bf16[2048,3,256]{2,1,0:T(4,128)(2,1)} fusion(bf16[2048,3,256]{2,1,0:T(4,128)(2,1)} %pad_maximum_fusion.3, s32[2048]{0:T(1024)S(1)} %copy-done.24), kind=kCustom, calls=%fused_computation.3 | custom fusion | bytes 6299648 | tf_op jit(solution)/shard_map/gather | solution.py:209
  705.4 51.6 %all_to_all.60 = bf16[2048,3,1,256]{3,1,2,0:T(4,128)(2,1)S(1)} all-to-all(bf16[2048,3,1,256]{3,1,2,0:T(4,128)(2,1)} %bitcast.215), channel_id=1, replica_groups=mesh['seq'=4,'fsdp'=8] {'seq'}, dimensions={0} | all-to-all | bytes 6291456 | tf_op jit(solution)/shard_map/all_to_all | solution.py:210
  760.2 8.5 convolution_convert_fusion.1
  770.4 16.9 %convolution_convert_fusion = bf16[1024,8192]{1,0:T(8,128)(2,1)} fusion(bf16[512,4096]{1,0:T(8,128)(2,1)} %get-tuple-element.387, bf16[512,4096]{1,0:T(8,128)(2,1)} %get-tuple-element.386, f32[512,1024]{1,0:T(8,128)S(1)} %copy-done.12, f32[1024]{0:T(1024)S(1)} %bitcast.239, f32[512]{0:T(512)S(1)} %copy-done.35), kind=kOutput, calls=%fused_computation.63 | convolution fusion | flops 8616673280 | bytes 27269120 | tf_op jit(solution)/shard_map/rd,rf->df/dot_general | solution.py:139
  791.0 44.4 %reduce-scatter.7.cloned.1.call-done = bf16[128,3072]{1,0:T(8,128)(2,1)} async-done(((bf16[1024,3072]{1,0:T(8,128)(2,1)}), bf16[128,3072]{1,0:T(8,128)(2,1)}) %reduce-scatter.7.cloned.1.call-update) | async-done | bytes 786448 | tf_op jit(solution)/shard_map/reduce_scatter | solution.py:223
  835.4 169.0 %reduce-scatter.11.cloned.1.call-done = bf16[128,8192]{1,0:T(8,128)(2,1)} async-done(((bf16[1024,8192]{1,0:T(8,128)(2,1)}), bf16[128,8192]{1,0:T(8,128)(2,1)}) %reduce-scatter.11.cloned.1.call-update) | async-done | bytes 2097168 | tf_op jit(solution)/shard_map/reduce_scatter | solution.py:234
  1004.5 10.3 fusion.69
  1014.8 8.1 fusion.66
  1022.9 13.9 %all-reduce.2 = (bf16[1024]{0:T(1024)(128)(2,1)S(1)}, bf16[1024]{0:T(1024)(128)(2,1)S(1)}) all-reduce(bf16[1024]{0:T(1024)(128)(2,1)S(1)} %get-tuple-element.327, bf16[1024]{0:T(1024)(128)(2,1)S(1)} %copy-done.37), channel_id=3, replica_groups=mesh['seq'=4,'fsdp'=8] {'fsdp'}, use_global_device_ids=true, to_apply=%region_14.15.clone | all-reduce | flops 2048 | bytes 8192
  1037.0 10.5 all-reduce.3
  1051.6 6.4 all-gather.17.cloned.1.call-done
  1058.0 6.9 reshape.372
  1064.9 23.0 %reduce_sum.100 = bf16[128,4096]{0,1:T(8,128)(2,1)S(1)} reduce(bf16[4,128,4096]{1,0,2:T(4,128)(2,1)} %reshape.372, bf16[]{:T(256)} %constant.60.clone.1), dimensions={0}, to_apply=%region_26.27 | reduce | flops 1572864 | bytes 5242882 | tf_op jit(solution)/shard_map/reduce_sum | solution.py:247
  1089.5 59.3 %all-reduce.7.cloned.1.call-done = (bf16[128,3072]{1,0:T(8,128)(2,1)}, bf16[128,1024]{1,0:T(8,128)(2,1)}, bf16[128,8192]{1,0:T(8,128)(2,1)}) async-done(((bf16[128,3072]{1,0:T(8,128)(2,1)}, bf16[128,1024]{1,0:T(8,128)(2,1)}, bf16[128,8192]{1,0:T(8,128)(2,1)}), (bf16[128,3072]{1,0:T(8,128)(2,1)}, bf16[128,1024]{1,0:T(8,128)(2,1)}, bf16[128,8192]{1,0:T(8,128)(2,1)})) %all-reduce.7.cloned.1.call-update) | async-done | bytes 3145744 | tf_op jit(solution)/shard_map/psum | solution.py:243
  (288 shorter events, 190.4 us)
Async XLA Ops:
  7.2 70.6 %all-gather.9.cloned.1.call-start = ((), (), s32[]{:S(2)}) async-start(), calls=%async_computation.8 | async-start | bytes 7077888 | tf_op jit(solution)/shard_map/all_gather | solution.py:52
  9.6 296.0 %all-gather.11.cloned.1.call-start = ((), (), s32[]{:S(2)}) async-start(), calls=%async_computation.9 | async-start | bytes 2359296 | tf_op jit(solution)/shard_map/all_gather | solution.py:53
  11.5 17.4 %copy-start.7 = (bf16[1,512,1024]{2,1,0:T(8,128)(2,1)S(1)}, bf16[1,512,1024]{2,1,0:T(8,128)(2,1)}, u32[]{:S(2)}) copy-start(bf16[1,512,1024]{2,1,0:T(8,128)(2,1)} %param.15) | copy-start | bytes 3145732
  11.5 298.6 %all-gather.13.cloned.1.call-start = ((), (), s32[]{:S(2)}) async-start(), calls=%async_computation.10 | async-start | bytes 18874368 | tf_op jit(solution)/shard_map/all_gather | solution.py:111
  28.9 48.8 %copy-start.29 = (f32[8,1,128]{2,1,0:T(1,128)}, f32[8,1,128]{2,1,0:T(1,128)S(1)}, u32[]{:S(2)}) copy-start(f32[8,1,128]{2,1,0:T(1,128)S(1)} %convert_element_type.216) | copy-start | bytes 12292
  29.8 47.9 %copy-start.32 = (f32[512]{0:T(512)}, f32[512]{0:T(512)S(1)}, u32[]{:S(2)}) copy-start(f32[512]{0:T(512)S(1)} %get-tuple-element.393) | copy-start | bytes 6148
  95.2 6.7 copy-start.38
  95.2 6.7 copy-start.40
  95.2 7.4 copy-start.36
  95.2 40.6 %all-to-all-start = ((bf16[512,3,4,256]{0,3,1,2:T(8,128)(2,1)}), bf16[512,3,4,256]{0,3,1,2:T(8,128)(2,1)S(1)}, u32[]{:S(2)}, u32[]{:S(2)}) async-start(bf16[512,3,4,256]{0,3,1,2:T(8,128)(2,1)} %copy.111), calls=%async_computation | async-start | bytes 6291456 | tf_op jit(solution)/shard_map/all_to_all | solution.py:58
  99.1 243.2 %all-gather.15.cloned.1.call-start = ((), (), s32[]{:S(2)}) async-start(), calls=%async_computation.11 | async-start | bytes 9437184 | tf_op jit(solution)/shard_map/all_gather | solution.py:112
  112.0 41.5 %copy-start.25 = (s32[2048]{0:T(1024)}, s32[2048]{0:T(1024)S(1)}, u32[]{:S(2)}) copy-start(s32[2048]{0:T(1024)S(1)} %fusion.84) | copy-start | bytes 24580
  256.1 8.6 copy-start.23
  273.7 9.2 copy-start.41
  278.6 17.8 %all-to-all-start.1 = ((bf16[4,2,65536]{2,1,0:T(2,128)(2,1)}), bf16[4,2,65536]{2,1,0:T(2,128)(2,1)}, u32[]{:S(2)}, u32[]{:S(2)}) async-start(bf16[4,2,65536]{2,1,0:T(2,128)(2,1)} %reshape.394), calls=%async_computation.1 | async-start | bytes 2097152 | tf_op jit(solution)/shard_map/all_to_all | solution.py:105
  282.9 504.5 %reduce-scatter.13.cloned.1.call-start = ((), (), s32[]{:S(2)}) async-start(), calls=%async_computation.16 | async-start | bytes 9437184
  292.7 103.3 %copy-start.27 = (f32[8,1,128]{2,1,0:T(1,128)}, f32[8,1,128]{2,1,0:T(1,128)S(1)}, u32[]{:S(2)}) copy-start(f32[8,1,128]{2,1,0:T(1,128)S(1)} %convert_element_type.217) | copy-start | bytes 12292
  292.7 12.9 %copy-start.8 = (bf16[1,512,1024]{2,1,0:T(8,128)(2,1)S(1)}, bf16[1,512,1024]{2,1,0:T(8,128)(2,1)}, u32[]{:S(2)}) copy-start(bf16[1,512,1024]{2,1,0:T(8,128)(2,1)} %param.15) | copy-start | bytes 3145732
  310.1 85.8 %copy-start.34 = (f32[512]{0:T(512)}, f32[512]{0:T(512)S(1)}, u32[]{:S(2)}) copy-start(f32[512]{0:T(512)S(1)} %get-tuple-element.395) | copy-start | bytes 6148
  310.2 32.1 %copy-start.22 = (bf16[1,512,1024]{2,1,0:T(8,128)(2,1)S(1)}, bf16[1,512,1024]{2,1,0:T(8,128)(2,1)}, u32[]{:S(2)}) copy-start(bf16[1,512,1024]{2,1,0:T(8,128)(2,1)} %param.22) | copy-start | bytes 3145732
  402.9 17.9 %all-to-all-start.2 = ((bf16[512,4,256]{0,2,1:T(8,128)(2,1)}), bf16[512,4,256]{0,2,1:T(8,128)(2,1)S(1)}, u32[]{:S(2)}, u32[]{:S(2)}) async-start(bf16[512,4,256]{0,2,1:T(8,128)(2,1)} %bitcast.224), calls=%async_computation.2 | async-start | bytes 2097152 | tf_op jit(solution)/shard_map/all_to_all | solution.py:159
  406.6 384.4 %reduce-scatter.9.cloned.1.call-start = ((), (), s32[]{:S(2)}) async-start(), calls=%async_computation.13 | async-start | bytes 2359296 | tf_op jit(solution)/shard_map/reduce_scatter | solution.py:226
  411.1 13.9 %copy-start.26 = (s32[2048]{0:T(1024)S(1)}, s32[2048]{0:T(1024)}, u32[]{:S(2)}) copy-start(s32[2048]{0:T(1024)} %copy-done.25) | copy-start | bytes 24580
  411.1 424.3 %reduce-scatter.7.cloned.1.call-start = ((), (), s32[]{:S(2)}) async-start(), calls=%async_computation.12 | async-start | bytes 7077888 | tf_op jit(solution)/shard_map/reduce_scatter | solution.py:223
  450.8 15.8 %copy-start = (f32[4,512,2048]{2,1,0:T(8,128)}, f32[4,512,2048]{2,1,0:T(8,128)S(1)}, u32[]{:S(2)}) copy-start(f32[4,512,2048]{2,1,0:T(8,128)S(1)} %fusion.146) | copy-start | bytes 50331652 | tf_op jit(solution)/shard_map/while
  477.5 6.7 copy-start.17
  477.5 15.3 %slice-start = ((s8[8388608]{0:T(1024)(128)(4,1)}), s8[4194304]{0:T(1024)(128)(4,1)S(1)}, s32[]{:S(2)}) async-start(s8[8388608]{0:T(1024)(128)(4,1)} %bitcast.213), calls=%async_computation.18 | async-start | bytes 8388608 | tf_op jit(solution)/shard_map/while
  484.2 8.6 slice-start.1
  492.8 5.4 copy-start.18
  492.9 5.4 copy-start.2
  492.9 5.4 copy-start.6
  492.9 5.4 copy-start.21
  502.6 15.8 %copy-start = (f32[4,512,2048]{2,1,0:T(8,128)}, f32[4,512,2048]{2,1,0:T(8,128)S(1)}, u32[]{:S(2)}) copy-start(f32[4,512,2048]{2,1,0:T(8,128)S(1)} %fusion.146) | copy-start | bytes 50331652 | tf_op jit(solution)/shard_map/while
  529.4 7.2 copy-start.17
  529.4 15.7 %slice-start = ((s8[8388608]{0:T(1024)(128)(4,1)}), s8[4194304]{0:T(1024)(128)(4,1)S(1)}, s32[]{:S(2)}) async-start(s8[8388608]{0:T(1024)(128)(4,1)} %bitcast.213), calls=%async_computation.18 | async-start | bytes 8388608 | tf_op jit(solution)/shard_map/while
  536.6 8.5 slice-start.1
  545.1 5.4 copy-start.18
  545.1 5.4 copy-start.2
  545.1 5.4 copy-start.6
  554.9 15.8 %copy-start = (f32[4,512,2048]{2,1,0:T(8,128)}, f32[4,512,2048]{2,1,0:T(8,128)S(1)}, u32[]{:S(2)}) copy-start(f32[4,512,2048]{2,1,0:T(8,128)S(1)} %fusion.146) | copy-start | bytes 50331652 | tf_op jit(solution)/shard_map/while
  581.6 7.2 copy-start.17
  581.6 15.7 %slice-start = ((s8[8388608]{0:T(1024)(128)(4,1)}), s8[4194304]{0:T(1024)(128)(4,1)S(1)}, s32[]{:S(2)}) async-start(s8[8388608]{0:T(1024)(128)(4,1)} %bitcast.213), calls=%async_computation.18 | async-start | bytes 8388608 | tf_op jit(solution)/shard_map/while
  588.8 8.5 slice-start.1
  597.3 5.4 copy-start.18
  597.3 5.4 copy-start.2
  597.3 5.4 copy-start.6
  607.1 15.8 %copy-start = (f32[4,512,2048]{2,1,0:T(8,128)}, f32[4,512,2048]{2,1,0:T(8,128)S(1)}, u32[]{:S(2)}) copy-start(f32[4,512,2048]{2,1,0:T(8,128)S(1)} %fusion.146) | copy-start | bytes 50331652 | tf_op jit(solution)/shard_map/while
  633.8 7.2 copy-start.17
  633.8 15.7 %slice-start = ((s8[8388608]{0:T(1024)(128)(4,1)}), s8[4194304]{0:T(1024)(128)(4,1)S(1)}, s32[]{:S(2)}) async-start(s8[8388608]{0:T(1024)(128)(4,1)} %bitcast.213), calls=%async_computation.18 | async-start | bytes 8388608 | tf_op jit(solution)/shard_map/while
  641.0 8.5 slice-start.1
  649.5 5.4 copy-start.18
  649.5 5.4 copy-start.2
  649.5 5.4 copy-start.6
  655.2 5.7 copy-start.3
  664.7 12.4 %copy-start.13 = (bf16[2048,1,256]{2,1,0:T(2,128)(2,1)S(1)}, bf16[2048,1,256]{2,1,0:T(2,128)(2,1)}, u32[]{:S(2)}) copy-start(bf16[2048,1,256]{2,1,0:T(2,128)(2,1)} %copy.133) | copy-start | bytes 3145732
  677.1 9.5 copy-start.24
  768.8 235.6 %reduce-scatter.11.cloned.1.call-start = ((), (), s32[]{:S(2)}) async-start(), calls=%async_computation.14 | async-start | bytes 18874368 | tf_op jit(solution)/shard_map/reduce_scatter | solution.py:234
  787.3 270.7 %all-gather.17.cloned.1.call-start = ((), (), s32[]{:S(2)}) async-start(), calls=%async_computation.15 | async-start | bytes 5242880 | tf_op jit(solution)/shard_map/all_gather | solution.py:247
  789.7 359.1 %all-reduce.7.cloned.1.call-start = ((), (), s32[]{:S(2)}) async-start(), calls=%async_computation.17 | async-start | bytes 6291456 | tf_op jit(solution)/shard_map/psum | solution.py:243
  1004.4 10.3 copy-start.9
  1004.5 10.3 copy-start.15
  1014.8 8.1 copy-start.37
  1014.8 33.7 %copy-start.11 = (f32[512,1024]{1,0:T(8,128)S(1)}, f32[512,1024]{1,0:T(8,128)}, u32[]{:S(2)}) copy-start(f32[512,1024]{1,0:T(8,128)} %copy-done.10) | copy-start | bytes 6291460
  1014.8 33.7 %copy-start.31 = (f32[512]{0:T(512)S(1)}, f32[512]{0:T(512)}, u32[]{:S(2)}) copy-start(f32[512]{0:T(512)} %get-tuple-element.392) | copy-start | bytes 6148
  (28 other events, 85.2 us)
Sparse Core Ops, SparseCore 0:
  10.2 67.4 all-gather.8
  79.9 27.7 all-gather.10
  109.3 150.5 all-gather.12
  261.9 80.2 all-gather.14
  377.9 88.1 reduce-scatter.12
  468.2 34.1 reduce-scatter.8
  768.9 66.4 reduce-scatter.6
  837.8 166.5 reduce-scatter.10
  1006.8 51.1 all-gather.16
  1061.2 87.5 all-reduce.6
